TPU v7x, 256 devices: a whole 4x4x8 slice. The times are simulated.
256 devices in a mesh: band: 64 (over z, y, x_lo), slab: 4 (over x_hi, core).
Axes of the slice: x: 4 (x_hi: 2, x_lo: 2; x = x_hi * 2 + x_lo), y: 4, z: 8, core: 2. Of those that a mesh axis runs over, the one named last changes fastest.
Arguments:
- bands: float32 [256, 32, 24, 128], P('band', 'slab'), may hold values from -8 to 8
- potential: float32 [32, 24, 128], P('slab'), may hold values from -1 to 0
Outputs:
- filtered: float32 [256, 32, 24, 128], P('band', 'slab')
- correlation: float32 [256, 256], P('band')
- projected: float32 [256, 256], P('band')
All inputs are finite; a program needn't handle non-finite values.
Results may differ from a plain program's by a relative error of at most 0.000092.
Values sent between devices are 32-bit elements; how exact they have to be, the bound alone decides.
No kernel may reach another device: no remote copies, remote signals or barrier semaphores. Data moves between devices by JAX's collectives and lax.ppermute only.
A program may use at most 128 MiB of HBM per device.

v0:
```python
import jax
import jax.numpy as jnp
from jax import lax
from jax.sharding import PartitionSpec as P

centre = 4.5
half = 3.5


def extended(block, sides, width):
    for axis, dim in sides:
        count = lax.axis_size(axis)
        forward = [(i, i + 1) for i in range(count - 1)]
        forward.append((count - 1, 0))
        backward = [(target, source) for source, target in forward]
        low = lax.ppermute(
            lax.slice_in_dim(block, block.shape[dim] - width, None, axis=dim), axis, forward
        )
        high = lax.ppermute(lax.slice_in_dim(block, 0, width, axis=dim), axis, backward)
        block = jnp.concatenate([low, block, high], axis=dim)
    return block


def hamiltonian(field, potential):
    padded = extended(field, (("slab", 1),), 2)
    middle = padded[:, 2:-2]
    lap = (
        -2.5 * middle
        + 4.0 / 3.0 * (padded[:, 1:-3] + padded[:, 3:-1])
        - 1.0 / 12.0 * (padded[:, :-4] + padded[:, 4:])
    )
    for axis in (2, 3):
        lap = lap - 2.5 * middle
        lap = lap + 4.0 / 3.0 * (jnp.roll(middle, 1, axis) + jnp.roll(middle, -1, axis))
        lap = lap - 1.0 / 12.0 * (jnp.roll(middle, 2, axis) + jnp.roll(middle, -2, axis))
    return -0.5 * lap + potential[None] * middle


def body(bands, potential):
    previous = bands
    current = (hamiltonian(bands, potential) - centre * bands) / half
    for step in range(3):
        following = 2.0 * (hamiltonian(current, potential) - centre * current) / half - previous
        previous, current = (current, following)
    image = hamiltonian(current, potential)
    local_bands = current.shape[0]
    volume = 1.0 / (current.shape[1] * lax.axis_size("slab") * current.shape[2] * current.shape[3])
    flat = current.reshape(local_bands, -1)
    himage = image.reshape(local_bands, -1)
    piece = lax.all_gather(current, "band", axis=0, tiled=True)
    others = piece.reshape(piece.shape[0], -1)
    gram_part = jnp.dot(
        flat, others.T, precision=lax.Precision.HIGHEST, preferred_element_type=jnp.float32
    )
    proj_part = jnp.dot(
        himage, others.T, precision=lax.Precision.HIGHEST, preferred_element_type=jnp.float32
    )
    gram_total, proj_total = lax.psum((gram_part, proj_part), "slab")
    return (current, gram_total * volume, proj_total * volume)


def solution(mesh):
    in_specs = (P("band", "slab", None, None), P("slab", None, None))
    out_specs = (P("band", "slab", None, None), P("band", None), P("band", None))
    return jax.shard_map(body, mesh=mesh, in_specs=in_specs, out_specs=out_specs, check_vma=False)
```

profile of v0, /device:TPU:8, one launch (start us, length us, event | category | flops | bytes accessed | tf_op | source)
XLA Modules:
  0.0 698.7 jit_solution(11574022964327537829)
XLA Ops:
  7.2 1.0 fusion.155
  8.3 3.2 collective-permute-start.1
  11.6 1.3 fusion.163
  12.9 1.2 fusion.157
  14.1 1.2 fusion.159
  15.3 1.3 fusion.160
  16.6 1.3 fusion.161
  18.0 1.3 fusion.162
  19.3 1.0 fusion.158
  21.2 1.0 fusion.156
  22.2 1.1 constant_dynamic-update-slice_fusion
  23.3 1.8 broadcast_multiply_fusion
  26.1 3.2 collective-permute-start.3
  29.3 2.3 collective-permute-done.2
  33.4 3.1 collective-permute-start.4
  37.0 2.2 collective-permute-done.4
  40.9 3.1 collective-permute-start.6
  44.1 14.4 %collective-permute-start.7 = (f32[4,2,24,128]{3,2,1,0:T(8,128)S(1)}, f32[4,2,24,128]{3,2,1,0:T(8,128)S(1)}, u32[]{:S(2)}, u32[]{:S(2)}) collective-permute-start(f32[4,2,24,128]{3,2,1,0:T(8,128)S(1)} %get-tuple-element.45), channel_id=1, source_target_pairs={{1,0},{2,1},{3,2},{0,3},{5,4},{6,5},{7,6},{4,7},{9,8},{10,9},{11,1... | collective-permute-start | bytes 294920 | tf_op jit(solution)/shard_map/ppermute | solution.py:19
  58.5 2.2 collective-permute-done.7
  60.7 1.5 fusion.39
  63.2 3.0 collective-permute-start.8
  67.7 1.3 fusion.119
  68.9 1.3 fusion.120
  70.2 1.3 fusion.121
  71.5 1.3 fusion.122
  72.8 1.2 fusion.123
  74.0 1.2 fusion.125
  76.2 2.3 fusion.22
  78.5 534.0 %all-gather.2.cloned.1.call-done = f32[256,8,24,128]{3,2,1,0:T(8,128)} async-done(((f32[4,8,24,128]{3,2,1,0:T(8,128)}), f32[256,8,24,128]{3,2,1,0:T(8,128)}) %all-gather.2.cloned.1.call-update) | async-done | bytes 25165840 | tf_op jit(solution)/shard_map/all_gather | solution.py:50
  612.5 39.1 %fusion.4 = f32[4,256]{1,0:T(4,128)S(1)} fusion(f32[256,8,24,128]{3,2,1,0:T(8,128)} %all-gather.2.cloned.1.call-done, f32[4,8,24,128]{3,2,1,0:T(8,128)} %fusion.39), kind=kOutput, calls=%fused_computation.4 | convolution fusion | flops 301989888 | bytes 25563136 | tf_op jit(solution)/shard_map/dot_general | solution.py:52
  651.6 30.1 %fusion.7 = f32[4,256]{1,0:T(4,128)S(1)} fusion(f32[256,8,24,128]{3,2,1,0:T(8,128)} %all-gather.2.cloned.1.call-done, f32[4,8,24,128]{3,2,1,0:T(8,128)S(1)} %fusion.22), kind=kOutput, calls=%fused_computation.5 | convolution fusion | flops 301989888 | bytes 25563136 | tf_op jit(solution)/shard_map/dot_general | solution.py:55
  681.6 9.2 %all-reduce = (f32[4,256]{1,0:T(4,128)S(1)}, f32[4,256]{1,0:T(4,128)S(1)}) all-reduce(f32[4,256]{1,0:T(4,128)S(1)} %fusion.4, f32[4,256]{1,0:T(4,128)S(1)} %fusion.7), channel_id=1, replica_groups=mesh['band'=64,'slab'=4] {'slab'}, use_global_device_ids=true, to_apply=%region_0.1 | all-reduce | flops 2048 | bytes 16384 | tf_op jit(solution)/shard_map/psum | solution.py:58
  (53 shorter events, 10.1 us)
Async XLA Ops:
  7.2 24.5 %copy-start = (f32[4,8,24,128]{3,2,1,0:T(8,128)S(1)}, f32[4,8,24,128]{3,2,1,0:T(8,128)}, u32[]{:S(2)}) copy-start(f32[4,8,24,128]{3,2,1,0:T(8,128)} %param.2) | copy-start | bytes 1179652
  7.2 32.1 %copy-start.1 = (f32[8,24,128]{2,1,0:T(8,128)S(1)}, f32[8,24,128]{2,1,0:T(8,128)}, u32[]{:S(2)}) copy-start(f32[8,24,128]{2,1,0:T(8,128)} %param.3) | copy-start | bytes 294916
  7.2 605.3 %all-gather.2.cloned.1.call-start = ((), (), s32[]{:S(2)}) async-start(), calls=%async_computation | async-start | bytes 25559040 | tf_op jit(solution)/shard_map/all_gather | solution.py:50
  8.2 13.9 %collective-permute-start = (f32[4,2,24,128]{3,2,1,0:T(8,128)S(1)}, f32[4,2,24,128]{3,2,1,0:T(8,128)S(1)}, u32[]{:S(2)}, u32[]{:S(2)}) collective-permute-start(f32[4,2,24,128]{3,2,1,0:T(8,128)S(1)} %get-tuple-element.84), channel_id=1, source_target_pairs={{0,1},{1,2},{2,3},{3,0},{4,5},{5,6},{6,7},{7,4},{8,9},{9,10},{10,1... | collective-permute-start | bytes 294920 | tf_op jit(solution)/shard_map/ppermute | solution.py:16
  8.3 14.9 %collective-permute-start.1 = (f32[4,2,24,128]{3,2,1,0:T(8,128)S(1)}, f32[4,2,24,128]{3,2,1,0:T(8,128)S(1)}, u32[]{:S(2)}, u32[]{:S(2)}) collective-permute-start(f32[4,2,24,128]{3,2,1,0:T(8,128)S(1)} %get-tuple-element.85), channel_id=1, source_target_pairs={{1,0},{2,1},{3,2},{0,3},{5,4},{6,5},{7,6},{4,7},{9,8},{10,9},{11,1... | collective-permute-start | bytes 294920 | tf_op jit(solution)/shard_map/ppermute | solution.py:19
  26.0 5.6 collective-permute-start.2
  26.1 5.6 collective-permute-start.3
  33.4 5.8 collective-permute-start.4
  36.5 2.7 collective-permute-start.5
  40.9 17.6 %collective-permute-start.6 = (f32[4,2,24,128]{3,2,1,0:T(8,128)S(1)}, f32[4,2,24,128]{3,2,1,0:T(8,128)S(1)}, u32[]{:S(2)}, u32[]{:S(2)}) collective-permute-start(f32[4,2,24,128]{3,2,1,0:T(8,128)S(1)} %get-tuple-element.44), channel_id=1, source_target_pairs={{0,1},{1,2},{2,3},{3,0},{4,5},{5,6},{6,7},{7,4},{8,9},{9,10},{10,1... | collective-permute-start | bytes 294920 | tf_op jit(solution)/shard_map/ppermute | solution.py:16
  44.1 16.6 %collective-permute-start.7 = (f32[4,2,24,128]{3,2,1,0:T(8,128)S(1)}, f32[4,2,24,128]{3,2,1,0:T(8,128)S(1)}, u32[]{:S(2)}, u32[]{:S(2)}) collective-permute-start(f32[4,2,24,128]{3,2,1,0:T(8,128)S(1)} %get-tuple-element.45), channel_id=1, source_target_pairs={{1,0},{2,1},{3,2},{0,3},{5,4},{6,5},{7,6},{4,7},{9,8},{10,9},{11,1... | collective-permute-start | bytes 294920 | tf_op jit(solution)/shard_map/ppermute | solution.py:19
  63.2 13.0 %collective-permute-start.8 = (f32[4,2,24,128]{3,2,1,0:T(8,128)S(1)}, f32[4,2,24,128]{3,2,1,0:T(8,128)S(1)}, u32[]{:S(2)}, u32[]{:S(2)}) collective-permute-start(f32[4,2,24,128]{3,2,1,0:T(8,128)S(1)} %get-tuple-element.26), channel_id=1, source_target_pairs={{0,1},{1,2},{2,3},{3,0},{4,5},{5,6},{6,7},{7,4},{8,9},{9,10},{10,1... | collective-permute-start | bytes 294920 | tf_op jit(solution)/shard_map/ppermute | solution.py:16
  66.2 10.0 %collective-permute-start.9 = (f32[4,2,24,128]{3,2,1,0:T(8,128)S(1)}, f32[4,2,24,128]{3,2,1,0:T(8,128)S(1)}, u32[]{:S(2)}, u32[]{:S(2)}) collective-permute-start(f32[4,2,24,128]{3,2,1,0:T(8,128)S(1)} %get-tuple-element.27), channel_id=1, source_target_pairs={{1,0},{2,1},{3,2},{0,3},{5,4},{6,5},{7,6},{4,7},{9,8},{10,9},{11,1... | collective-permute-start | bytes 294920 | tf_op jit(solution)/shard_map/ppermute | solution.py:19
Sparse Core Ops, SparseCore 0:
  62.3 550.1 all-gather.1
where the time goes:
time: 707 us; the launch traced here: 699 us
  waiting for transfers between devices  541 us (77%)
  matrix products  69.1 us (10%)
  starting transfers between devices  31.3 us (4%)
  local copies, waits for them, and re-layouts  24.9 us (4%)
  between operations  14.7 us (2%)
  blocking collectives  9.23 us (1%)
  other arithmetic  8.61 us (1%)
    all_gather x1, waiting for transfers between devices, body(): piece = lax.all_gather(current, 'band', axis=0, tiled=True)  534 us
    dot_general x1, matrix products, body(): jnp.dot(flat, others.T, precision=lax.Precision.HIGHEST, preferred_elemen...  39.1 us
    dot_general x1, matrix products, body(): jnp.dot(himage, others.T, precision=lax.Precision.HIGHEST, preferred_elem...  30.1 us
    ppermute x5, starting transfers between devices, extended(): lax.ppermute(lax.slice_in_dim(block, 0, width, axis=dim), axis, backward)  21.8 us
  transfers between devices with their start and end apart: 11, of which 6 were waited for; matrix products, arithmetic and copies ran while one was open for 4% of the time, Pallas kernels for 0%

commit v1 on v0

--- a/solution.py
+++ b/solution.py
@@ -47,7 +47,9 @@
     volume = 1.0 / (current.shape[1] * lax.axis_size("slab") * current.shape[2] * current.shape[3])
     flat = current.reshape(local_bands, -1)
     himage = image.reshape(local_bands, -1)
-    piece = lax.all_gather(current, "band", axis=0, tiled=True)
+    piece = jnp.concatenate(
+        lax.all_to_all(jnp.stack([current] * lax.axis_size("band")), "band", 0, 0), axis=0
+    )
     others = piece.reshape(piece.shape[0], -1)
     gram_part = jnp.dot(
         flat, others.T, precision=lax.Precision.HIGHEST, preferred_element_type=jnp.float32

time: 707 us -> 773 us (1.093)
  the two profiles are of different devices: /device:TPU:8 before, /device:TPU:100 now
where the time goes in v1:
time: 773 us; the launch traced here: 772 us
  waiting for transfers between devices  609 us (79%)
  local copies, waits for them, and re-layouts  50.1 us (6%)
  matrix products  45.4 us (6%)
  blocking collectives  41.9 us (5%)
  starting transfers between devices  18.2 us (2%)
    all_to_all x1, waiting for transfers between devices, body(): lax.all_to_all(jnp.stack([current] * lax.axis_size('band')), 'band', 0, 0)  499 us
    ppermute x5, waiting for transfers between devices, extended(): lax.ppermute(lax.slice_in_dim(block, 0, width, axis=dim), axis, backward)  76.3 us
    psum x1, blocking collectives, body(): gram_total, proj_total = lax.psum((gram_part, proj_part), 'slab')  41.9 us
    ppermute x5, waiting for transfers between devices, extended(): lax.ppermute(lax.slice_in_dim(block, block.shape[dim] - width, None, axis...  33.8 us
    another operation x1, local copies, waits for them, and re-layouts, body(): others = piece.reshape(piece.shape[0], -1)  23.4 us
    dot_general x1, matrix products, body(): jnp.dot(himage, others.T, precision=lax.Precision.HIGHEST, preferred_elem...  22.7 us
    dot_general x1, matrix products, body(): jnp.dot(flat, others.T, precision=lax.Precision.HIGHEST, preferred_elemen...  22.7 us
  transfers between devices with their start and end apart: 11, of which 9 were waited for; matrix products, arithmetic and copies ran while one was open for 2% of the time, Pallas kernels for 0%

profile of v1, /device:TPU:100, one launch (start us, length us, event | category | flops | bytes accessed | tf_op | source)
XLA Modules:
  0.0 772.1 jit_solution(1925167266462359557)
XLA Ops:
  0.7 1.0 fusion.149
  1.8 3.2 collective-permute-start.1
  5.0 1.3 fusion.156
  6.3 1.3 fusion.157
  7.6 1.3 fusion.154
  8.8 1.3 fusion.155
  10.1 1.0 fusion.152
  11.1 1.2 fusion.153
  12.3 1.2 fusion.151
  13.5 0.9 broadcast_multiply_fusion.1
  14.4 1.0 fusion.150
  15.4 1.1 constant_dynamic-update-slice_fusion
  16.5 1.8 broadcast_multiply_fusion
  19.8 2.6 collective-permute-done.3
  22.4 2.5 collective-permute-done.2
  26.6 1.3 collective-permute-start.5
  27.9 3.0 collective-permute-done.5
  30.9 2.5 collective-permute-done.4
  33.5 0.8 fusion.46
  35.1 1.0 collective-permute-start.7
  36.2 3.2 collective-permute-done.7
  39.4 2.4 collective-permute-done.6
  42.5 11.5 %stack.2 = f32[64,4,8,24,128]{4,3,2,1,0:T(8,128)} broadcast(f32[4,8,24,128]{3,2,1,0:T(8,128)S(1)} %fusion.29), dimensions={1,2,3,4} | broadcast | bytes 25559040 | tf_op jit(solution)/shard_map/stack | solution.py:51
  54.0 11.1 %all-to-all-start = ((f32[64,4,8,24,128]{4,3,2,1,0:T(8,128)}), f32[64,4,8,24,128]{4,3,2,1,0:T(8,128)}, u32[]{:S(2)}, u32[]{:S(2)}) async-start(f32[64,4,8,24,128]{4,3,2,1,0:T(8,128)} %stack.2), calls=%async_computation | async-start | bytes 50331648 | tf_op jit(solution)/shard_map/all_to_all | solution.py:51
  65.1 0.8 collective-permute-start.9
  66.8 67.5 %collective-permute-done.9 = f32[4,2,24,128]{3,2,1,0:T(8,128)S(1)} collective-permute-done((f32[4,2,24,128]{3,2,1,0:T(8,128)S(1)}, f32[4,2,24,128]{3,2,1,0:T(8,128)S(1)}, u32[]{:S(2)}, u32[]{:S(2)}) %collective-permute-start.9) | collective-permute-done | bytes 98336 | tf_op jit(solution)/shard_map/ppermute | solution.py:19
  134.3 26.5 %collective-permute-done.8 = f32[4,2,24,128]{3,2,1,0:T(8,128)S(1)} collective-permute-done((f32[4,2,24,128]{3,2,1,0:T(8,128)S(1)}, f32[4,2,24,128]{3,2,1,0:T(8,128)S(1)}, u32[]{:S(2)}, u32[]{:S(2)}) %collective-permute-start.8) | collective-permute-done | bytes 98336 | tf_op jit(solution)/shard_map/ppermute | solution.py:16
  161.5 499.3 %all-to-all-done = f32[64,4,8,24,128]{4,3,2,1,0:T(8,128)} async-done(((f32[64,4,8,24,128]{4,3,2,1,0:T(8,128)}), f32[64,4,8,24,128]{4,3,2,1,0:T(8,128)}, u32[]{:S(2)}, u32[]{:S(2)}) %all-to-all-start) | async-done | bytes 25165856 | tf_op jit(solution)/shard_map/all_to_all | solution.py:51
  660.8 23.4 %reshape_reshape.3 = f32[256,24576]{1,0:T(8,128)} reshape(f32[64,4,8,24,128]{4,3,2,1,0:T(8,128)} %all-to-all-done) | data formatting | bytes 50331648 | tf_op jit(solution)/shard_map/reshape;reshape | solution.py:53
  684.2 22.7 %fusion.68 = f32[4,256]{1,0:T(4,128)S(1)} fusion(f32[256,24576]{1,0:T(8,128)} %reshape_reshape.3, f32[1,4,192,128]{3,2,1,0:T(8,128)S(1)} %bitcast.14), kind=kOutput, calls=%fused_computation.84 | convolution fusion | flops 301989888 | bytes 25563136 | tf_op jit(solution)/shard_map/dot_general | solution.py:54
  706.9 22.7 %fusion.65 = f32[4,256]{1,0:T(4,128)S(1)} fusion(f32[256,24576]{1,0:T(8,128)} %reshape_reshape.3, f32[1,4,192,128]{3,2,1,0:T(8,128)S(1)} %bitcast.15), kind=kOutput, calls=%fused_computation.81 | convolution fusion | flops 301989888 | bytes 25563136 | tf_op jit(solution)/shard_map/dot_general | solution.py:57
  729.6 41.9 %all-reduce = (f32[4,256]{1,0:T(4,128)S(1)}, f32[4,256]{1,0:T(4,128)S(1)}) all-reduce(f32[4,256]{1,0:T(4,128)S(1)} %fusion.68, f32[4,256]{1,0:T(4,128)S(1)} %fusion.65), channel_id=1, replica_groups=mesh['band'=64,'slab'=4] {'slab'}, use_global_device_ids=true, to_apply=%region_0.1 | all-reduce | flops 2048 | bytes 16384 | tf_op jit(solution)/shard_map/psum | solution.py:60
  (56 shorter events, 7.1 us)
Async XLA Ops:
  0.6 24.3 %copy-start.1 = (f32[4,8,24,128]{3,2,1,0:T(8,128)S(1)}, f32[4,8,24,128]{3,2,1,0:T(8,128)}, u32[]{:S(2)}) copy-start(f32[4,8,24,128]{3,2,1,0:T(8,128)} %param.2) | copy-start | bytes 1179652
  0.6 32.8 %copy-start.2 = (f32[8,24,128]{2,1,0:T(8,128)S(1)}, f32[8,24,128]{2,1,0:T(8,128)}, u32[]{:S(2)}) copy-start(f32[8,24,128]{2,1,0:T(8,128)} %param.3) | copy-start | bytes 294916
  1.7 13.7 %collective-permute-start = (f32[4,2,24,128]{3,2,1,0:T(8,128)S(1)}, f32[4,2,24,128]{3,2,1,0:T(8,128)S(1)}, u32[]{:S(2)}, u32[]{:S(2)}) collective-permute-start(f32[4,2,24,128]{3,2,1,0:T(8,128)S(1)} %get-tuple-element.81), channel_id=1, source_target_pairs={{0,1},{1,2},{2,3},{3,0},{4,5},{5,6},{6,7},{7,4},{8,9},{9,10},{10,1... | collective-permute-start | bytes 294920 | tf_op jit(solution)/shard_map/ppermute | solution.py:16
  1.8 14.7 %collective-permute-start.1 = (f32[4,2,24,128]{3,2,1,0:T(8,128)S(1)}, f32[4,2,24,128]{3,2,1,0:T(8,128)S(1)}, u32[]{:S(2)}, u32[]{:S(2)}) collective-permute-start(f32[4,2,24,128]{3,2,1,0:T(8,128)S(1)} %get-tuple-element.82), channel_id=1, source_target_pairs={{1,0},{2,1},{3,2},{0,3},{5,4},{6,5},{7,6},{4,7},{9,8},{10,9},{11,1... | collective-permute-start | bytes 294920 | tf_op jit(solution)/shard_map/ppermute | solution.py:19
  19.2 3.3 collective-permute-start.3
  19.3 5.6 collective-permute-start.2
  26.6 4.3 collective-permute-start.5
  27.9 5.5 collective-permute-start.4
  35.1 4.2 collective-permute-start.7
  36.2 5.5 collective-permute-start.6
  42.5 641.7 %copy-start = (f32[4,8,24,128]{3,2,1,0:T(8,128)}, f32[4,8,24,128]{3,2,1,0:T(8,128)S(1)}, u32[]{:S(2)}) copy-start(f32[4,8,24,128]{3,2,1,0:T(8,128)S(1)} %fusion.29) | copy-start | bytes 1179652
  54.0 606.8 %all-to-all-start = ((f32[64,4,8,24,128]{4,3,2,1,0:T(8,128)}), f32[64,4,8,24,128]{4,3,2,1,0:T(8,128)}, u32[]{:S(2)}, u32[]{:S(2)}) async-start(f32[64,4,8,24,128]{4,3,2,1,0:T(8,128)} %stack.2), calls=%async_computation | async-start | bytes 50331648 | tf_op jit(solution)/shard_map/all_to_all | solution.py:51
  65.1 69.3 %collective-permute-start.9 = (f32[4,2,24,128]{3,2,1,0:T(8,128)S(1)}, f32[4,2,24,128]{3,2,1,0:T(8,128)S(1)}, u32[]{:S(2)}, u32[]{:S(2)}) collective-permute-start(f32[4,2,24,128]{3,2,1,0:T(8,128)S(1)} %get-tuple-element.24), channel_id=1, source_target_pairs={{1,0},{2,1},{3,2},{0,3},{5,4},{6,5},{7,6},{4,7},{9,8},{10,9},{11,1... | collective-permute-start | bytes 294920 | tf_op jit(solution)/shard_map/ppermute | solution.py:19
  65.9 94.9 %collective-permute-start.8 = (f32[4,2,24,128]{3,2,1,0:T(8,128)S(1)}, f32[4,2,24,128]{3,2,1,0:T(8,128)S(1)}, u32[]{:S(2)}, u32[]{:S(2)}) collective-permute-start(f32[4,2,24,128]{3,2,1,0:T(8,128)S(1)} %get-tuple-element.23), channel_id=1, source_target_pairs={{0,1},{1,2},{2,3},{3,0},{4,5},{5,6},{6,7},{7,4},{8,9},{9,10},{10,1... | collective-permute-start | bytes 294920 | tf_op jit(solution)/shard_map/ppermute | solution.py:16
